TPU v7x, 256 devices: a whole 4x4x8 slice. The times are simulated.
256 devices in a mesh: ep: 64 (over z, y, core), dp: 4 (over x).
Axes of the slice: x: 4, y: 4, z: 8, core: 2. Of those that a mesh axis runs over, the one named last changes fastest.
Arguments:
- master_weight: float32 [128, 3584, 128], P('ep', 'dp'), may hold values from -3 to 3
- first_moment: float32 [128, 3584, 128], P('ep', 'dp'), may hold values from -2 to 2
- second_moment: float32 [128, 3584, 128], P('ep', 'dp'), may hold values from 0.05 to 2
- grad_owned: bfloat16 [4, 128, 3584, 128], P('dp', 'ep'), may hold values from -2.5 to 2.5
- grad_replica: bfloat16 [4, 128, 3584, 128], P('dp', 'ep'), may hold values from -2.5 to 2.5
- old_experts: int32 [128], replicated, may hold values from 0 to 127, each once
- new_experts: int32 [128], replicated, may hold values from 0 to 127, each once
- rep_expert: int32 [128], replicated, may hold values from 0 to 127
- rep_count: int32 [64], replicated, may hold values from 0 to 2, as said below
Outputs:
- new_weight: float32 [128, 3584, 128], P('ep', 'dp')
- new_first: float32 [128, 3584, 128], P('ep', 'dp')
- new_second: float32 [128, 3584, 128], P('ep', 'dp')
Inputs may be any that keep to these rules, and one draw needn't show every extreme that they name: `old_experts`: each expert appears once. `new_experts`: each expert appears once. The first rep_count[i] of the 2 replica slots of ep index i are live; some index has all live and some none.
All inputs are finite; a program needn't handle non-finite values.
Results may differ from a plain program's by a relative error of at most 0.0003.
Values may be sent and summed in bfloat16 or wider, within the bound.
A program may use at most 64 MiB of HBM per device.

v0:
```python
import jax
import jax.numpy as jnp
from jax import lax
from jax.experimental import pallas as pl
from jax.experimental.pallas import tpu as pltpu
from jax.sharding import PartitionSpec as P

beta_first = 0.9
beta_second = 0.95
learn_rate = 0.01
decay_rate = 0.1
adam_eps = 1e-08
corr_first = 1.0 - 0.9**10
corr_second = 1.0 - 0.95**10


def adam_update(weight_now, first_now, second_now, gradient):
    moved_first = beta_first * first_now + (1.0 - beta_first) * gradient
    moved_second = beta_second * second_now + (1.0 - beta_second) * gradient * gradient
    step_size = moved_first / corr_first / (jnp.sqrt(moved_second / corr_second) + adam_eps)
    moved_weight = weight_now - learn_rate * (step_size + decay_rate * weight_now)
    return (moved_weight, moved_first, moved_second)


def spread_kernel(w, f, s, go, gr, sw, sf, ss, ro, rr, ep_sems, dp_sems, own_sems):
    states, pieces, grads, blocks = (w, f, s), (sw, sf, ss), (go, gr), (ro, rr)
    count = lax.axis_size("ep")
    dp_count = lax.axis_size("dp")
    exp_dev = w.shape[0]
    piece = w.shape[1] // count
    rows = w.shape[1]
    me = lax.axis_index("ep")
    row = lax.axis_index("dp")
    mesh_id = pl.DeviceIdType.MESH

    def window(ref, owner):
        return ref.at[:, pl.ds(owner * piece, piece), :]

    def slots(ref, source):
        return ref.at[pl.ds(source * exp_dev, exp_dev)]

    def band(ref, target):
        return ref.at[:, pl.ds(target * rows, rows), :]

    barrier = pltpu.get_barrier_semaphore()

    def greet(k, carry):
        pl.semaphore_signal(
            barrier, inc=1, device_id=(lax.rem(me + k, count), row), device_id_type=mesh_id
        )
        return carry

    lax.fori_loop(1, count, greet, 0)
    for shift in range(1, dp_count):
        pl.semaphore_signal(
            barrier, inc=1, device_id=(me, (row + shift) % dp_count), device_id_type=mesh_id
        )
    pl.semaphore_wait(barrier, count - 1 + dp_count - 1)

    def dp_copy(b, shift, send_target):
        return pltpu.make_async_remote_copy(
            src_ref=band(grads[b], send_target),
            dst_ref=blocks[b].at[shift - 1],
            send_sem=dp_sems.at[b, 0, shift],
            recv_sem=dp_sems.at[b, 1, shift],
            device_id=(me, send_target),
            device_id_type=mesh_id,
        )

    local = []
    for a in range(3):
        copy = pltpu.make_async_copy(window(states[a], me), slots(pieces[a], me), own_sems.at[a])
        copy.start()
        local.append(copy)

    def ep_copy(a, k, peer, source):
        return pltpu.make_async_remote_copy(
            src_ref=window(states[a], peer),
            dst_ref=slots(pieces[a], source),
            send_sem=ep_sems.at[a, 0, k],
            recv_sem=ep_sems.at[a, 1, k],
            device_id=(peer, row),
            device_id_type=mesh_id,
        )

    def send(k, carry):
        peer = lax.rem(me + k, count)
        for a in range(3):
            ep_copy(a, k, peer, me).start()
        return carry

    lax.fori_loop(1, count, send, 0)
    for shift in range(1, dp_count):
        for b in range(2):
            dp_copy(b, shift, (row + shift) % dp_count).start()

    def finish(k, carry):
        peer = lax.rem(me + k, count)
        source = lax.rem(me + count - k, count)
        for a in range(3):
            ep_copy(a, k, peer, me).wait_send()
            ep_copy(a, k, peer, source).wait_recv()
        return carry

    lax.fori_loop(1, count, finish, 0)
    for shift in range(1, dp_count):
        for b in range(2):
            copy = dp_copy(b, shift, (row + shift) % dp_count)
            copy.wait_send()
            copy.wait_recv()
    for copy in local:
        copy.wait()


def spread(w, f, s, go, gr):
    count, dp_count = 64, 4
    exp_dev, rows, lanes = w.shape
    piece = rows // count
    state_out = jax.ShapeDtypeStruct((exp_dev * count, piece, lanes), w.dtype)
    grad_out = jax.ShapeDtypeStruct((dp_count - 1, go.shape[0], rows, lanes), go.dtype)
    size = 3 * w.size * w.dtype.itemsize + 2 * go.size * go.dtype.itemsize
    return pl.pallas_call(
        spread_kernel,
        out_shape=(state_out, state_out, state_out, grad_out, grad_out),
        in_specs=[pl.BlockSpec(memory_space=pl.ANY)] * 5,
        out_specs=tuple(pl.BlockSpec(memory_space=pl.ANY) for _ in range(5)),
        scratch_shapes=[
            pltpu.SemaphoreType.DMA((3, 2, count)),
            pltpu.SemaphoreType.DMA((2, 2, dp_count)),
            pltpu.SemaphoreType.DMA((3,)),
        ],
        compiler_params=pltpu.CompilerParams(collective_id=0, has_side_effects=True),
        cost_estimate=pl.CostEstimate(flops=0, transcendentals=0, bytes_accessed=2 * size),
    )(w, f, s, go, gr)


def per_device_body(
    master_weight,
    first_moment,
    second_moment,
    grad_owned,
    grad_replica,
    old_experts,
    new_experts,
    rep_expert,
    rep_count,
):
    ep_count = lax.axis_size("ep")
    exp_dev, shard_rows, columns = master_weight.shape
    rep_dev = grad_replica.shape[1]
    piece_rows = shard_rows // ep_count
    experts = exp_dev * ep_count
    replica_slots = rep_dev * ep_count

    dp_count = lax.axis_size("dp")
    dp_index = lax.axis_index("dp")
    sw, sf, ss, ro, rr = spread(
        master_weight, first_moment, second_moment, grad_owned[0], grad_replica[0]
    )

    def block_of(array, index):
        return lax.dynamic_slice_in_dim(array, index * shard_rows, shard_rows, axis=1)

    own_block = [block_of(grad_owned[0], dp_index), block_of(grad_replica[0], dp_index)]
    received = [[ro[i], rr[i]] for i in range(dp_count - 1)]
    sums = [part.astype(jnp.float32) for part in own_block]
    for got in received:
        sums = [total + part.astype(jnp.float32) for total, part in zip(sums, got)]
    grads = jnp.concatenate(sums, axis=0)
    source_index = jnp.sum(
        jnp.where(
            new_experts[:, None] == old_experts[None, :], lax.iota(jnp.int32, experts)[None, :], 0
        ),
        axis=1,
    )
    state_new = [jnp.take(x, source_index, axis=0) for x in (sw, sf, ss)]

    grads_p = lax.all_to_all(
        grads.reshape(exp_dev + rep_dev, ep_count, piece_rows, columns).transpose(1, 0, 2, 3),
        "ep",
        split_axis=0,
        concat_axis=0,
        tiled=True,
    )
    grads_p = grads_p.reshape(ep_count * (exp_dev + rep_dev), piece_rows * columns)

    column = lax.iota(jnp.int32, ep_count * (exp_dev + rep_dev))
    device_of, within = column // (exp_dev + rep_dev), column % (exp_dev + rep_dev)
    is_owned = within < exp_dev
    old_slot = jnp.clip(device_of * exp_dev + within, 0, experts - 1)
    rep_slot = jnp.clip(device_of * rep_dev + within - exp_dev, 0, replica_slots - 1)
    live = (rep_slot % rep_dev < rep_count[rep_slot // rep_dev]).astype(jnp.float32)
    column_expert = jnp.where(is_owned, old_experts[old_slot], rep_expert[rep_slot])
    column_weight = jnp.where(is_owned, jnp.float32(1.0), live)
    combine = jnp.where(
        new_experts[:, None] == column_expert[None, :], column_weight[None, :], jnp.float32(0.0)
    )
    gradient = jnp.dot(
        combine,
        grads_p,
        precision=lax.Precision.HIGHEST,
        preferred_element_type=jnp.float32,
    ).reshape(experts, piece_rows, columns)
    moved = jnp.stack(adam_update(state_new[0], state_new[1], state_new[2], gradient))
    back = lax.all_to_all(
        moved.reshape(3, ep_count, exp_dev, piece_rows, columns).transpose(1, 0, 2, 3, 4),
        "ep",
        split_axis=0,
        concat_axis=0,
        tiled=True,
    )
    back = back.transpose(1, 2, 0, 3, 4).reshape(3, exp_dev, shard_rows, columns)
    return (back[0], back[1], back[2])


def solution(mesh):
    in_specs = (
        P("ep", "dp", None),
        P("ep", "dp", None),
        P("ep", "dp", None),
        P("dp", "ep", None, None),
        P("dp", "ep", None, None),
        P(),
        P(),
        P(),
        P(),
    )
    out_specs = (P("ep", "dp", None), P("ep", "dp", None), P("ep", "dp", None))
    return jax.shard_map(
        per_device_body, mesh=mesh, in_specs=in_specs, out_specs=out_specs, check_vma=False
    )
```

profile of v0, /device:TPU:1, one launch (start us, length us, event | category | flops | bytes accessed | tf_op | source)
XLA Modules:
  0.0 224.5 jit_solution(9991700168839809229)
XLA Ops:
  0.6 0.0 copy-start
  0.7 76.0 %shard_map.112 = (f32[128,14,128]{2,1,0:T(8,128)}, f32[128,14,128]{2,1,0:T(8,128)}, f32[128,14,128]{2,1,0:T(8,128)}, bf16[3,2,896,128]{3,2,1,0:T(8,128)(2,1)}, bf16[3,2,896,128]{3,2,1,0:T(8,128)(2,1)}) custom-call(f32[2,896,128]{2,1,0:T(8,128)} %w.1, f32[2,896,128]{2,1,0:T(8,128)} %f.1, f32[2,896,128]{2,1,0:T(8,128)} %s.1, bf16[2,3584,128]{2,1,0:T(8,128)(2,1)} %bitcast.43, ...), custom_call_target="tpu_custom_call" | custom-call | bytes 12845056 | tf_op jit(solution)/shard_map/pallas_call | solution.py:122
  76.7 2.4 %convert_add_fusion = (f32[1,2,896,128]{3,2,1,0:T(8,128)S(1)}, f32[1,2,896,128]{3,2,1,0:T(8,128)S(1)}) fusion(bf16[3,2,896,128]{3,2,1,0:T(8,128)(2,1)} %get-tuple-element.12, bf16[1,2,3584,128]{3,2,1,0:T(8,128)(2,1)} %param.15, s32[]{:T(128)S(6)} %select_n.164, bf16[3,2,896,128]{3,2,1,0:T(8,128)(2,1)} %get-tuple-element.11, bf16[1,2,3584,128]{3,2,1,0:T(8,128)(2,1)} %param.14), kind=kLoop, calls=%fused_computation.16 | loop fusion | flops 3211264 | bytes 5505028 | tf_op jit(solution)/shard_map/add | solution.py:168
  79.1 0.7 copy.44
  79.8 0.7 copy.45
  80.5 2.1 maximum_bitcast_fusion.1
  82.6 0.0 copy-start.1
  82.6 0.0 copy-start.5
  82.6 11.7 %all-to-all-start = ((f32[64,4,14,128]{3,1,2,0:T(4,128)}), f32[64,4,14,128]{3,1,2,0:T(4,128)S(1)}, u32[]{:S(2)}, u32[]{:S(2)}) async-start(f32[64,4,14,128]{3,1,2,0:T(4,128)} %maximum_bitcast_fusion.1), calls=%async_computation | async-start | bytes 3670016 | tf_op jit(solution)/shard_map/all_to_all | solution.py:178
  94.4 0.0 copy-done.1
  94.4 1.9 gather_fusion
  96.2 0.0 copy-done.5
  96.2 0.2 select_reduce_fusion
  96.4 1.9 gather_fusion.3
  98.3 2.9 %gather_fusion.4 = f32[128,14,128]{2,1,0:T(8,128)} fusion(f32[128,14,128]{2,1,0:T(8,128)} %get-tuple-element.10, s32[1024]{0:T(1024)S(1)} %pad_clamp_fusion.3), kind=kCustom, calls=%fused_computation.1.clone | custom fusion | bytes 1835520 | tf_op jit(solution)/shard_map/jit(_take)/gather | solution.py:176
  101.2 0.0 copy-start.2
  101.2 2.8 %gather_fusion.5 = f32[128,14,128]{2,1,0:T(8,128)} fusion(f32[128,14,128]{2,1,0:T(8,128)} %get-tuple-element.13, s32[1024]{0:T(1024)S(1)} %pad_clamp_fusion.3), kind=kCustom, calls=%fused_computation.2.clone | custom fusion | bytes 1835520 | tf_op jit(solution)/shard_map/jit(_take)/gather | solution.py:176
  104.1 0.0 copy-done
  104.1 1.9 gather_fusion.1
  106.0 0.0 copy-done.2
  106.0 1.9 gather_fusion.2
  107.9 30.8 %all-to-all-done = f32[64,4,14,128]{3,1,2,0:T(4,128)S(1)} async-done(((f32[64,4,14,128]{3,1,2,0:T(4,128)}), f32[64,4,14,128]{3,1,2,0:T(4,128)S(1)}, u32[]{:S(2)}, u32[]{:S(2)}) %all-to-all-start) | async-done | bytes 1835040 | tf_op jit(solution)/shard_map/all_to_all | solution.py:178
  138.7 0.3 copy.46
  139.0 2.0 copy.67
  141.0 1.8 copy.47
  142.8 0.0 copy-start.3
  142.8 0.0 copy-start.4
  142.9 2.0 fusion.2
  144.9 0.0 copy-done.3
  144.9 0.0 copy-done.4
  144.9 1.3 multiply_subtract_fusion
  146.2 0.5 copy.51
  146.7 0.5 copy.52
  147.2 0.5 copy.53
  147.7 1.2 maximum_bitcast_fusion
  148.9 71.7 %all_to_all.10 = f32[64,3,2,14,128]{4,2,3,1,0:T(2,128)S(1)} all-to-all(f32[64,3,2,14,128]{4,2,3,1,0:T(2,128)S(1)} %maximum_bitcast_fusion), channel_id=1, replica_groups=mesh['ep'=64,'dp'=4] {'ep'}, dimensions={0} | all-to-all | bytes 5505024 | tf_op jit(solution)/shard_map/all_to_all | solution.py:205
  220.6 0.9 fusion.21
  221.5 1.0 copy.54
  222.5 1.0 copy.55
  223.5 1.0 copy.56
  (11 shorter events, 0.1 us)
Async XLA Ops:
  0.6 103.4 %copy-start = (s32[128]{0:T(128)S(1)}, s32[128]{0:T(128)}, u32[]{:S(2)}) copy-start(s32[128]{0:T(128)} %param.18) | copy-start | bytes 1540
  82.6 11.7 %copy-start.1 = (s32[128]{0:T(128)S(1)}, s32[128]{0:T(128)}, u32[]{:S(2)}) copy-start(s32[128]{0:T(128)} %param.16) | copy-start | bytes 1540
  82.6 13.6 %copy-start.5 = (s32[128]{0:T(128)S(1)}, s32[128]{0:T(128)}, u32[]{:S(2)}) copy-start(s32[128]{0:T(128)} %param.17) | copy-start | bytes 1540
  82.6 56.1 %all-to-all-start = ((f32[64,4,14,128]{3,1,2,0:T(4,128)}), f32[64,4,14,128]{3,1,2,0:T(4,128)S(1)}, u32[]{:S(2)}, u32[]{:S(2)}) async-start(f32[64,4,14,128]{3,1,2,0:T(4,128)} %maximum_bitcast_fusion.1), calls=%async_computation | async-start | bytes 3670016 | tf_op jit(solution)/shard_map/all_to_all | solution.py:178
  101.2 4.8 %copy-start.2 = (s32[64]{0:T(128)S(1)}, s32[64]{0:T(128)}, u32[]{:S(2)}) copy-start(s32[64]{0:T(128)} %param.19) | copy-start | bytes 772
  142.8 2.1 copy-start.3
  142.8 2.1 copy-start.4
where the time goes:
time: 225 us; the launch traced here: 224 us
  Pallas kernels  76 us (34%)
  blocking collectives  71.7 us (32%)
  waiting for transfers between devices  30.8 us (14%)
  local copies, waits for them, and re-layouts  24 us (11%)
  starting transfers between devices  11.7 us (5%)
  other arithmetic  7.26 us (3%)
    pallas_call x1, Pallas kernels, spread(): pl.pallas_call(spread_kernel, out_shape=(state_out, state_out, state_out,...  76 us
    all_to_all x1, blocking collectives, per_device_body(): lax.all_to_all(moved.reshape(3, ep_count, exp_dev, piece_rows, columns).t...  71.7 us
    all_to_all x1, waiting for transfers between devices, per_device_body(): lax.all_to_all(grads.reshape(exp_dev + rep_dev, ep_count, piece_rows, col...  30.8 us
    all_to_all x1, starting transfers between devices, per_device_body(): lax.all_to_all(grads.reshape(exp_dev + rep_dev, ep_count, piece_rows, col...  11.7 us
    gather x3, local copies, waits for them, and re-layouts, per_device_body(): state_new = [jnp.take(x, source_index, axis=0) for x in (sw, sf, ss)]  7.58 us
    unnamed x16, local copies, waits for them, and re-layouts  4.99 us
  transfers between devices with their start and end apart: 1, of which 1 were waited for; matrix products, arithmetic and copies ran while one was open for 6% of the time, Pallas kernels for 0%

commit v1 on v0

--- a/solution.py
+++ b/solution.py
@@ -122,14 +122,17 @@
     return pl.pallas_call(
         spread_kernel,
         out_shape=(state_out, state_out, state_out, grad_out, grad_out),
-        in_specs=[pl.BlockSpec(memory_space=pl.ANY)] * 5,
+        in_specs=[pl.BlockSpec(memory_space=pltpu.VMEM)] * 3
+        + [pl.BlockSpec(memory_space=pl.ANY)] * 2,
         out_specs=tuple(pl.BlockSpec(memory_space=pl.ANY) for _ in range(5)),
         scratch_shapes=[
             pltpu.SemaphoreType.DMA((3, 2, count)),
             pltpu.SemaphoreType.DMA((2, 2, dp_count)),
             pltpu.SemaphoreType.DMA((3,)),
         ],
-        compiler_params=pltpu.CompilerParams(collective_id=0, has_side_effects=True),
+        compiler_params=pltpu.CompilerParams(
+            collective_id=0, has_side_effects=True, vmem_limit_bytes=32 * 1024 * 1024
+        ),
         cost_estimate=pl.CostEstimate(flops=0, transcendentals=0, bytes_accessed=2 * size),
     )(w, f, s, go, gr)
 

time: 225 us -> 230 us (1.022)
  local copies, waits for them, and re-layouts: 24 us -> 28.8 us
  waiting for transfers between devices: 30.8 us -> 34 us
    unnamed x16 -> x26, local copies, waits for them, and re-layouts: 4.99 us -> 11.6 us
    gather x3, local copies, waits for them, and re-layouts: 7.58 us -> 4.26 us  [per_device_body(): state_new = [jnp.take(x, source_index, axis=0) for x in (sw, sf, ss)]]
    all_to_all x1, waiting for transfers between devices: 30.8 us -> 34 us  [per_device_body(): lax.all_to_all(grads.reshape(exp_dev + rep_dev, ep_count, piece_rows, col...]
  transfers between devices with their start and end apart: 1 -> 1, of which waited for: 1 -> 1; matrix products, arithmetic and copies ran while one was open for 6% -> 4% of each run, Pallas kernels for 0% -> 0%
where the time goes in v1:
time: 230 us
  Pallas kernels  75.2 us (33%)
  blocking collectives  71.7 us (31%)
  waiting for transfers between devices  34 us (15%)
  local copies, waits for them, and re-layouts  28.8 us (13%)
  starting transfers between devices  12 us (5%)
  other arithmetic  5.26 us (2%)
    pallas_call x1, Pallas kernels, spread(): pl.pallas_call(spread_kernel, out_shape=(state_out, state_out, state_out,...  75.2 us
    all_to_all x1, blocking collectives, per_device_body(): lax.all_to_all(moved.reshape(3, ep_count, exp_dev, piece_rows, columns).t...  71.7 us
    all_to_all x1, waiting for transfers between devices, per_device_body(): lax.all_to_all(grads.reshape(exp_dev + rep_dev, ep_count, piece_rows, col...  34 us
    all_to_all x1, starting transfers between devices, per_device_body(): lax.all_to_all(grads.reshape(exp_dev + rep_dev, ep_count, piece_rows, col...  12 us
    unnamed x26, local copies, waits for them, and re-layouts  11.6 us
  transfers between devices with their start and end apart: 1, of which 1 were waited for; matrix products, arithmetic and copies ran while one was open for 4% of the time, Pallas kernels for 0%

profile of v1, /device:TPU:1, one launch (start us, length us, event | category | flops | bytes accessed | tf_op | source)
XLA Modules:
  0.0 229.9 jit_solution(1183149762848647759)
XLA Ops:
  0.6 0.0 copy-start
  0.7 0.0 copy-start.1
  0.7 1.5 copy-done.1
  2.2 1.5 copy-done.2
  3.7 1.2 copy-done.3
  4.8 0.0 copy-start.4
  4.8 1.2 copy-done.4
  6.0 0.0 copy-start.5
  6.0 1.2 copy-done.5
  7.2 75.2 %shard_map.112 = (f32[128,14,128]{2,1,0:T(8,128)S(1)}, f32[128,14,128]{2,1,0:T(8,128)S(1)}, f32[128,14,128]{2,1,0:T(8,128)S(1)}, bf16[3,2,896,128]{3,2,1,0:T(8,128)(2,1)S(1)}, bf16[3,2,896,128]{3,2,1,0:T(8,128)(2,1)S(1)}) custom-call(f32[2,896,128]{2,1,0:T(8,128)S(1)} %copy-done.3, f32[2,896,128]{2,1,0:T(8,128)S(1)} %copy-done.4, ...), custom_call_target="tpu_custom_call" | custom-call | bytes 12845056 | tf_op jit(solution)/shard_map/pallas_call | solution.py:122
  82.4 0.4 convert_add_fusion
  82.8 0.7 copy.44
  83.5 0.7 copy.45
  84.3 2.1 maximum_bitcast_fusion.1
  86.3 0.0 copy-start.6
  86.3 0.0 copy-start.10
  86.3 12.0 %all-to-all-start = ((f32[64,4,14,128]{3,1,2,0:T(4,128)}), f32[64,4,14,128]{3,1,2,0:T(4,128)}, u32[]{:S(2)}, u32[]{:S(2)}) async-start(f32[64,4,14,128]{3,1,2,0:T(4,128)} %maximum_bitcast_fusion.1), calls=%async_computation | async-start | bytes 3670016 | tf_op jit(solution)/shard_map/all_to_all | solution.py:181
  98.4 0.0 copy-done.6
  98.4 1.9 gather_fusion
  100.2 0.0 copy-done.10
  100.3 0.2 select_reduce_fusion
  100.5 1.7 gather_fusion.3
  102.2 0.8 gather_fusion.4
  103.0 0.0 copy-start.7
  103.0 1.8 gather_fusion.5
  104.8 0.0 copy-done
  104.8 1.9 gather_fusion.1
  106.7 0.0 copy-done.7
  106.7 1.9 gather_fusion.2
  108.6 34.0 %all-to-all-done = f32[64,4,14,128]{3,1,2,0:T(4,128)} async-done(((f32[64,4,14,128]{3,1,2,0:T(4,128)}), f32[64,4,14,128]{3,1,2,0:T(4,128)}, u32[]{:S(2)}, u32[]{:S(2)}) %all-to-all-start) | async-done | bytes 1835040 | tf_op jit(solution)/shard_map/all_to_all | solution.py:181
  142.7 1.8 copy.46
  144.4 2.0 copy.67
  146.5 1.8 copy.47
  148.3 0.0 copy-start.8
  148.3 0.0 copy-start.9
  148.3 2.0 fusion.2
  150.4 0.0 copy-done.8
  150.4 0.0 copy-done.9
  150.4 1.3 multiply_subtract_fusion
  151.7 0.5 copy.51
  152.2 0.5 copy.52
  152.6 0.5 copy.53
  153.1 1.2 maximum_bitcast_fusion
  154.3 71.7 %all_to_all.10 = f32[64,3,2,14,128]{4,2,3,1,0:T(2,128)S(1)} all-to-all(f32[64,3,2,14,128]{4,2,3,1,0:T(2,128)S(1)} %maximum_bitcast_fusion), channel_id=1, replica_groups=mesh['ep'=64,'dp'=4] {'ep'}, dimensions={0} | all-to-all | bytes 5505024 | tf_op jit(solution)/shard_map/all_to_all | solution.py:208
  226.0 0.9 fusion.21
  227.0 1.0 copy.54
  228.0 1.0 copy.55
  229.0 1.0 copy.56
  (13 shorter events, 0.1 us)
Async XLA Ops:
  0.6 104.1 %copy-start = (s32[128]{0:T(128)S(1)}, s32[128]{0:T(128)}, u32[]{:S(2)}) copy-start(s32[128]{0:T(128)} %param.18) | copy-start | bytes 1540
  0.7 1.5 copy-start.1
  2.2 1.5 copy-start.2
  3.7 1.2 copy-start.3
  4.8 1.2 copy-start.4
  6.0 1.2 copy-start.5
  86.3 12.0 %copy-start.6 = (s32[128]{0:T(128)S(1)}, s32[128]{0:T(128)}, u32[]{:S(2)}) copy-start(s32[128]{0:T(128)} %param.16) | copy-start | bytes 1540
  86.3 13.9 %copy-start.10 = (s32[128]{0:T(128)S(1)}, s32[128]{0:T(128)}, u32[]{:S(2)}) copy-start(s32[128]{0:T(128)} %param.17) | copy-start | bytes 1540
  86.3 56.3 %all-to-all-start = ((f32[64,4,14,128]{3,1,2,0:T(4,128)}), f32[64,4,14,128]{3,1,2,0:T(4,128)}, u32[]{:S(2)}, u32[]{:S(2)}) async-start(f32[64,4,14,128]{3,1,2,0:T(4,128)} %maximum_bitcast_fusion.1), calls=%async_computation | async-start | bytes 3670016 | tf_op jit(solution)/shard_map/all_to_all | solution.py:181
  103.0 3.7 %copy-start.7 = (s32[64]{0:T(128)S(1)}, s32[64]{0:T(128)}, u32[]{:S(2)}) copy-start(s32[64]{0:T(128)} %param.19) | copy-start | bytes 772
  148.3 2.1 copy-start.8
  148.3 2.1 copy-start.9
